TPU v7x, 32 devices: a whole 2x2x4 slice. The times are simulated.
32 devices in a mesh: row: 4 (over z), col: 8 (over y, x, core).
Axes of the slice: x: 2, y: 2, z: 4, core: 2. Of those that a mesh axis runs over, the one named last changes fastest.
Arguments:
- image: float32 [16, 16, 64, 128], P('row', 'col'), may hold values from -6 to 6
- u_factors: bfloat16 [20, 16, 1024, 256], P('row', 'col'), may hold values from -0.125 to 0.125
- v_factors: bfloat16 [20, 16, 1024, 256], P('row', 'col'), may hold values from -0.1875 to 0.1875
- ranks: int32 [20, 16], P('row', 'col'), may hold values from 16 to 256
- measured: bfloat16 [20480, 128], P('row'), may hold values from -6 to 6
Outputs:
- new_image: float32 [16, 16, 64, 128], P('row', 'col')
All inputs are finite; a program needn't handle non-finite values.
Results may differ from a plain program's by a relative error of at most 0.0051.
Values may be sent and summed in bfloat16 or wider, within the bound.
No kernel may reach another device: no remote copies, remote signals or barrier semaphores. Data moves between devices by JAX's collectives and lax.ppermute only.
A program may use at most 128 MiB of HBM per device.

v0:
```python
import jax
import jax.numpy as jnp
from jax import lax
from jax.sharding import PartitionSpec as P

diff_rate = 0.12
edge_scale = 0.5


def padded_2(block, sides, width):
    for axis, dim in sides:
        count = lax.axis_size(axis)
        forward = [(i, i + 1) for i in range(count - 1)]
        backward = [(target, source) for source, target in forward]
        low = lax.ppermute(
            lax.slice_in_dim(block, block.shape[dim] - width, None, axis=dim), axis, forward
        )
        high = lax.ppermute(lax.slice_in_dim(block, 0, width, axis=dim), axis, backward)
        block = jnp.concatenate([low, block, high], axis=dim)
    return block


def flux(delta):
    scaled = delta / edge_scale
    return delta / (1.0 + scaled * scaled)


def diffuse_margin(extended):
    padded = jnp.pad(extended, ((0, 0), (0, 0), (1, 1), (0, 0)))
    center = padded[1:-1, 1:-1, 1:-1]
    total = flux(padded[2:, 1:-1, 1:-1] - center) + flux(padded[:-2, 1:-1, 1:-1] - center)
    total = total + flux(padded[1:-1, 2:, 1:-1] - center) + flux(padded[1:-1, :-2, 1:-1] - center)
    total = total + flux(padded[1:-1, 1:-1, 2:] - center) + flux(padded[1:-1, 1:-1, :-2] - center)
    return center + diff_rate * total


def body(image, u_factors, v_factors, ranks, measured):
    row_tiles, col_tiles, tile_len, rank_max = u_factors.shape
    frames = image.shape[3]
    local_x, local_y = (image.shape[0], image.shape[1])
    whole = lax.all_gather(image.astype(jnp.bfloat16), "row", axis=0, tiled=True)
    xtiles = whole.reshape(col_tiles, tile_len, frames)
    levels = lax.broadcasted_iota(jnp.int32, (row_tiles, col_tiles, rank_max), 2)
    mask = (levels < ranks[:, :, None]).astype(jnp.float32)
    coef = jnp.einsum("ijkr,jkf->ijrf", v_factors, xtiles, preferred_element_type=jnp.float32)
    coef = (coef * mask[:, :, :, None]).astype(jnp.bfloat16)
    partial_value = jnp.einsum(
        "ijkr,ijrf->ikf", u_factors, coef, preferred_element_type=jnp.float32
    )
    partial_value = partial_value.reshape(row_tiles * tile_len, frames)
    total = lax.psum(partial_value, "col")
    resid = (total - measured.astype(jnp.float32)).astype(jnp.bfloat16)
    resid = resid.reshape(row_tiles, tile_len, frames)
    back = jnp.einsum("ijkr,ikf->ijrf", u_factors, resid, preferred_element_type=jnp.float32)
    back = (back * mask[:, :, :, None]).astype(jnp.bfloat16)
    grad_terms = jnp.einsum("ijkr,ijrf->jkf", v_factors, back, preferred_element_type=jnp.float32)
    grad_terms = grad_terms.reshape(col_tiles * tile_len, frames)
    gradient = lax.psum_scatter(grad_terms, "row", scatter_dimension=0, tiled=True)
    moved = image - gradient.reshape(image.shape)
    extended = padded_2(moved, (("row", 0), ("col", 1)), 2)
    middle = diffuse_margin(extended)
    grid_x = local_x * lax.axis_size("row")
    grid_y = local_y * lax.axis_size("col")
    pos_x = (
        lax.broadcasted_iota(jnp.int32, (local_x + 2, 1, 1, 1), 0)
        + lax.axis_index("row") * local_x
        - 1
    )
    pos_y = (
        lax.broadcasted_iota(jnp.int32, (1, local_y + 2, 1, 1), 1)
        + lax.axis_index("col") * local_y
        - 1
    )
    inside = (pos_x >= 0) & (pos_x < grid_x) & ((pos_y >= 0) & (pos_y < grid_y))
    middle = jnp.where(inside, middle, 0.0)
    moved = diffuse_margin(middle)
    return moved


def solution(mesh):
    placed = (
        P("row", "col", None, None),
        P("row", "col", None, None),
        P("row", "col", None, None),
        P("row", "col"),
        P("row", None),
    )
    return jax.shard_map(
        body, mesh=mesh, in_specs=placed, out_specs=P("row", "col", None, None), check_vma=False
    )
```

profile of v0, /device:TPU:1, one launch (start us, length us, event | category | flops | bytes accessed | tf_op | source)
XLA Modules:
  0.0 176.0 jit_solution(7555312063323355615)
XLA Ops:
  6.5 0.8 copy.20
  7.3 0.1 compare_convert_fusion
  7.4 1.0 convert_element_type.29
  8.4 15.3 %all_gather.3 = bf16[16,2,64,128]{3,2,1,0:T(8,128)(2,1)S(1)} all-gather(bf16[4,2,64,128]{3,2,1,0:T(8,128)(2,1)S(1)} %convert_element_type.29), channel_id=1, replica_groups=mesh['row'=4,'col'=8] {'row'}, dimensions={0}, use_global_device_ids=true | all-gather | bytes 655360 | tf_op jit(solution)/shard_map/all_gather | solution.py:41
  23.7 6.6 %convolution_bitcast_fusion = f32[5,1024,128]{1,2,0:T(8,128)S(1)} fusion(bf16[5,2,1024,256]{3,2,1,0:T(8,128)(2,1)} %param.6, bf16[2,1024,128,1]{2,1,0,3:T(8,128)(2,1)S(1)} %bitcast.37, bf16[5,2,1024,256]{3,2,1,0:T(8,128)(2,1)} %param.7, f32[5,2,256]{2,1,0:T(2,128)S(1)} %compare_convert_fusion), kind=kOutput, calls=%fused_computation.7 | convolution fusion | flops 1342832640 | bytes 13641728 | tf_op jit(solution)/shard_map/ijkr,ijrf->ikf/dot_general | solution.py:47
  30.3 2.1 %copy.21 = f32[5,1024,128]{2,1,0:T(8,128)} copy(f32[5,1024,128]{1,2,0:T(8,128)S(1)} %convolution_bitcast_fusion) | data formatting | bytes 5242880 | tf_op jit(solution)/shard_map/ijkr,ijrf->ikf/dot_general | solution.py:47
  32.5 67.2 %all-reduce.4.cloned.1.call-done = f32[5120,128]{1,0:T(8,128)} async-done(((f32[5120,128]{1,0:T(8,128)}), f32[5120,128]{1,0:T(8,128)}) %all-reduce.4.cloned.1.call-update) | async-done | bytes 2621456 | tf_op jit(solution)/shard_map/psum | solution.py:51
  99.7 2.0 %subtract_convert_fusion = bf16[5120,128]{1,0:T(8,128)(2,1)S(1)} fusion(f32[5120,128]{1,0:T(8,128)} %all-reduce.4.cloned.1.call-done, bf16[5120,128]{1,0:T(8,128)(2,1)S(1)} %copy-done), kind=kLoop, calls=%fused_computation.4 | loop fusion | flops 1966080 | bytes 5242880 | tf_op jit(solution)/shard_map/convert_element_type | solution.py:52
  101.7 7.7 %fusion.8 = f32[2,1024,128]{1,2,0:T(8,128)} fusion(bf16[5,2,1024,256]{3,2,1,0:T(8,128)(2,1)} %param.7, bf16[5,1024,128,1]{2,1,0,3:T(8,128)(2,1)S(1)} %bitcast.38, bf16[5,2,1024,256]{3,2,1,0:T(8,128)(2,1)} %param.6, f32[5,2,256]{2,0,1:T(8,128)S(1)} %copy.24), kind=kOutput, calls=%fused_computation.12 | convolution fusion | flops 1342832640 | bytes 12855296 | tf_op jit(solution)/shard_map/ijkr,ijrf->jkf/dot_general | solution.py:56
  109.4 2.6 %copy.26 = f32[2,1024,128]{2,1,0:T(8,128)} copy(f32[2,1024,128]{1,2,0:T(8,128)} %fusion.8) | data formatting | bytes 2097152 | tf_op jit(solution)/shard_map/ijkr,ijrf->jkf/dot_general | solution.py:56
  112.0 27.3 %reduce-scatter.2.cloned.1.call-done = f32[512,128]{1,0:T(8,128)} async-done(((f32[2048,128]{1,0:T(8,128)}), f32[512,128]{1,0:T(8,128)}) %reduce-scatter.2.cloned.1.call-update) | async-done | bytes 262160 | tf_op jit(solution)/shard_map/reduce_scatter | solution.py:58
  139.3 1.0 sub.51
  140.3 1.3 collective-permute-start
  141.6 1.3 collective-permute-start.1
  142.9 0.6 collective-permute-done
  143.5 4.7 %collective-permute-done.1 = f32[2,2,64,128]{3,2,1,0:T(8,128)S(1)} collective-permute-done((f32[2,2,64,128]{3,2,1,0:T(8,128)S(1)}, f32[2,2,64,128]{3,2,1,0:T(8,128)S(1)}, u32[]{:S(2)}, u32[]{:S(2)}) %collective-permute-start.1) | collective-permute-done | bytes 131104 | tf_op jit(solution)/shard_map/ppermute | solution.py:18
  148.2 4.6 %collective-permute-start.2 = (f32[8,2,64,128]{3,2,1,0:T(8,128)S(1)}, f32[8,2,64,128]{3,2,1,0:T(8,128)S(1)}, u32[]{:S(2)}, u32[]{:S(2)}) collective-permute-start(f32[8,2,64,128]{3,2,1,0:T(8,128)S(1)} %pad_maximum_fusion.7), channel_id=1, source_target_pairs={{0,1},{1,2},{2,3},{3,4},{4,5},{5,6},{6,7},{8,9},{9,10},{10,11},{11... | collective-permute-start | bytes 1572872 | tf_op jit(solution)/shard_map/ppermute | solution.py:15
  152.9 1.9 %collective-permute-start.3 = (f32[8,2,64,128]{3,2,1,0:T(8,128)S(1)}, f32[8,2,64,128]{3,2,1,0:T(8,128)S(1)}, u32[]{:S(2)}, u32[]{:S(2)}) collective-permute-start(f32[8,2,64,128]{3,2,1,0:T(8,128)S(1)} %pad_maximum_fusion.7), channel_id=1, source_target_pairs={{1,0},{2,1},{3,2},{4,3},{5,4},{6,5},{7,6},{9,8},{10,9},{11,10},{12... | collective-permute-start | bytes 1572872 | tf_op jit(solution)/shard_map/ppermute | solution.py:18
  154.8 0.1 broadcast_and_fusion
  154.9 4.1 %collective-permute-done.2 = f32[8,2,64,128]{3,2,1,0:T(8,128)S(1)} collective-permute-done((f32[8,2,64,128]{3,2,1,0:T(8,128)S(1)}, f32[8,2,64,128]{3,2,1,0:T(8,128)S(1)}, u32[]{:S(2)}, u32[]{:S(2)}) %collective-permute-start.2) | collective-permute-done | bytes 524320 | tf_op jit(solution)/shard_map/ppermute | solution.py:15
  159.0 7.2 %collective-permute-done.3 = f32[8,2,64,128]{3,2,1,0:T(8,128)S(1)} collective-permute-done((f32[8,2,64,128]{3,2,1,0:T(8,128)S(1)}, f32[8,2,64,128]{3,2,1,0:T(8,128)S(1)}, u32[]{:S(2)}, u32[]{:S(2)}) %collective-permute-start.3) | collective-permute-done | bytes 524320 | tf_op jit(solution)/shard_map/ppermute | solution.py:18
  166.2 0.2 pad_maximum_fusion
  166.4 1.6 add_select_fusion
  168.0 1.1 multiply_add_fusion
  (13 shorter events, 0.2 us)
Async XLA Ops:
  6.5 93.1 %all-reduce.4.cloned.1.call-start = ((), (), s32[]{:S(2)}) async-start(), calls=%async_computation.1 | async-start | bytes 5242880 | tf_op jit(solution)/shard_map/psum | solution.py:51
  32.4 67.3 %copy-start = (bf16[5120,128]{1,0:T(8,128)(2,1)S(1)}, bf16[5120,128]{1,0:T(8,128)(2,1)}, u32[]{:S(2)}) copy-start(bf16[5120,128]{1,0:T(8,128)(2,1)} %param.9) | copy-start | bytes 3932164
  32.4 106.8 %reduce-scatter.2.cloned.1.call-start = ((), (), s32[]{:S(2)}) async-start(), calls=%async_computation.2 | async-start | bytes 1310720 | tf_op jit(solution)/shard_map/reduce_scatter | solution.py:58
  109.4 29.9 %copy-start.1 = (f32[4,2,64,128]{3,2,1,0:T(8,128)S(1)}, f32[4,2,64,128]{3,2,1,0:T(8,128)}, u32[]{:S(2)}) copy-start(f32[4,2,64,128]{3,2,1,0:T(8,128)} %param.5) | copy-start | bytes 786436
  140.3 3.2 %collective-permute-start = (f32[2,2,64,128]{3,2,1,0:T(8,128)S(1)}, f32[2,2,64,128]{3,2,1,0:T(8,128)S(1)}, u32[]{:S(2)}, u32[]{:S(2)}) collective-permute-start(f32[2,2,64,128]{3,2,1,0:T(8,128)S(1)} %get-tuple-element.5), channel_id=1, source_target_pairs={{0,8},{8,16},{16,24},{1,9},{9,17},{17,25},{2,10},{10,18},{18,26},{... | collective-permute-start | bytes 393224 | tf_op jit(solution)/shard_map/ppermute | solution.py:15
  141.6 6.6 %collective-permute-start.1 = (f32[2,2,64,128]{3,2,1,0:T(8,128)S(1)}, f32[2,2,64,128]{3,2,1,0:T(8,128)S(1)}, u32[]{:S(2)}, u32[]{:S(2)}) collective-permute-start(f32[2,2,64,128]{3,2,1,0:T(8,128)S(1)} %get-tuple-element.6), channel_id=1, source_target_pairs={{8,0},{16,8},{24,16},{9,1},{17,9},{25,17},{10,2},{18,10},{26,18},{... | collective-permute-start | bytes 393224 | tf_op jit(solution)/shard_map/ppermute | solution.py:18
  148.2 10.7 %collective-permute-start.2 = (f32[8,2,64,128]{3,2,1,0:T(8,128)S(1)}, f32[8,2,64,128]{3,2,1,0:T(8,128)S(1)}, u32[]{:S(2)}, u32[]{:S(2)}) collective-permute-start(f32[8,2,64,128]{3,2,1,0:T(8,128)S(1)} %pad_maximum_fusion.7), channel_id=1, source_target_pairs={{0,1},{1,2},{2,3},{3,4},{4,5},{5,6},{6,7},{8,9},{9,10},{10,11},{11... | collective-permute-start | bytes 1572872 | tf_op jit(solution)/shard_map/ppermute | solution.py:15
  152.9 13.3 %collective-permute-start.3 = (f32[8,2,64,128]{3,2,1,0:T(8,128)S(1)}, f32[8,2,64,128]{3,2,1,0:T(8,128)S(1)}, u32[]{:S(2)}, u32[]{:S(2)}) collective-permute-start(f32[8,2,64,128]{3,2,1,0:T(8,128)S(1)} %pad_maximum_fusion.7), channel_id=1, source_target_pairs={{1,0},{2,1},{3,2},{4,3},{5,4},{6,5},{7,6},{9,8},{10,9},{11,10},{12... | collective-permute-start | bytes 1572872 | tf_op jit(solution)/shard_map/ppermute | solution.py:18
Sparse Core Ops, SparseCore 0:
  32.6 67.0 all-reduce.3
  112.1 27.1 reduce-scatter.1
where the time goes:
time: 176 us
  waiting for transfers between devices  111 us (63%)
  blocking collectives  15.3 us (9%)
  matrix products  14.3 us (8%)
  between operations  13.5 us (8%)
  starting transfers between devices  9.15 us (5%)
  other arithmetic  7.07 us (4%)
  local copies, waits for them, and re-layouts  5.47 us (3%)
    psum x1, waiting for transfers between devices, body(): total = lax.psum(partial_value, 'col')  67.2 us
    reduce_scatter x1, waiting for transfers between devices, body(): lax.psum_scatter(grad_terms, 'row', scatter_dimension=0, tiled=True)  27.3 us
    all_gather x1, blocking collectives, body(): lax.all_gather(image.astype(jnp.bfloat16), 'row', axis=0, tiled=True)  15.3 us
    ppermute x2, waiting for transfers between devices, padded_2(): lax.ppermute(lax.slice_in_dim(block, 0, width, axis=dim), axis, backward)  11.9 us
    dot_general x1, matrix products, body(): jnp.einsum('ijkr,ijrf->jkf', v_factors, back, preferred_element_type=jnp....  7.72 us
    dot_general x1, matrix products, body(): jnp.einsum('ijkr,ijrf->ikf', u_factors, coef, preferred_element_type=jnp....  6.62 us
    ppermute x2, starting transfers between devices, padded_2(): lax.ppermute(lax.slice_in_dim(block, block.shape[dim] - width, None, axis...  5.9 us
    ppermute x2, waiting for transfers between devices, padded_2(): lax.ppermute(lax.slice_in_dim(block, block.shape[dim] - width, None, axis...  4.69 us
  transfers between devices with their start and end apart: 6, of which 6 were waited for; matrix products, arithmetic and copies ran while one was open for 0% of the time, Pallas kernels for 0%

commit v1 on v0

--- a/solution.py
+++ b/solution.py
@@ -38,7 +38,20 @@
     row_tiles, col_tiles, tile_len, rank_max = u_factors.shape
     frames = image.shape[3]
     local_x, local_y = (image.shape[0], image.shape[1])
-    whole = lax.all_gather(image.astype(jnp.bfloat16), "row", axis=0, tiled=True)
+    x = image.astype(jnp.bfloat16)
+    ways, here, hop = (lax.axis_size("row"), lax.axis_index("row"), x.shape[0])
+    dims = [n * ways if d == 0 else n for d, n in enumerate(x.shape)]
+    full = lax.dynamic_update_slice_in_dim(jnp.zeros(dims, x.dtype), x, here * hop, axis=0)
+    going_up = going_down = x
+    for far in range(1, ways // 2 + 1):
+        going_up = lax.ppermute(going_up, "row", [(d, (d + 1) % ways) for d in range(ways)])
+        full = lax.dynamic_update_slice_in_dim(full, going_up, (here - far) % ways * hop, axis=0)
+        if 2 * far < ways:
+            going_down = lax.ppermute(going_down, "row", [(d, (d - 1) % ways) for d in range(ways)])
+            full = lax.dynamic_update_slice_in_dim(
+                full, going_down, (here + far) % ways * hop, axis=0
+            )
+    whole = full
     xtiles = whole.reshape(col_tiles, tile_len, frames)
     levels = lax.broadcasted_iota(jnp.int32, (row_tiles, col_tiles, rank_max), 2)
     mask = (levels < ranks[:, :, None]).astype(jnp.float32)

time: 176 us -> 171 us (0.972); the launches traced: 176 us -> 168 us
  blocking collectives: 15.3 us -> 0 us
  starting transfers between devices: 9.15 us -> 13.4 us
  waiting for transfers between devices: 111 us -> 114 us
    all_gather x1 -> x0, blocking collectives: 15.3 us -> none  [body(): lax.all_gather(image.astype(jnp.bfloat16), 'row', axis=0, tiled=True)]
    ppermute x0 -> x3, waiting for transfers between devices: none -> 7.93 us  [the longest x2 5.52 us: body(): lax.ppermute(going_up, 'row', [(d, (d + 1) % ways) for d in range(ways)])]
    ppermute x0 -> x3, starting transfers between devices: none -> 4.26 us  [the longest x2 2.17 us: body(): lax.ppermute(going_up, 'row', [(d, (d + 1) % ways) for d in range(ways)])]
    ppermute x2, waiting for transfers between devices: 4.69 us -> 0.63 us  [padded_2(): lax.ppermute(lax.slice_in_dim(block, block.shape[dim] - width, None, axis...]
  transfers between devices with their start and end apart: 6 -> 9, of which waited for: 6 -> 8; matrix products, arithmetic and copies ran while one was open for 0% -> 1% of each run, Pallas kernels for 0% -> 0%
where the time goes in v1:
time: 171 us; the launch traced here: 168 us
  waiting for transfers between devices  114 us (67%)
  matrix products  14.3 us (8%)
  between operations  13.5 us (8%)
  starting transfers between devices  13.4 us (8%)
  other arithmetic  7.79 us (5%)
  local copies, waits for them, and re-layouts  4.91 us (3%)
    psum x1, waiting for transfers between devices, body(): total = lax.psum(partial_value, 'col')  65.9 us
    reduce_scatter x1, waiting for transfers between devices, body(): lax.psum_scatter(grad_terms, 'row', scatter_dimension=0, tiled=True)  27.3 us
    ppermute x2, waiting for transfers between devices, padded_2(): lax.ppermute(lax.slice_in_dim(block, 0, width, axis=dim), axis, backward)  12.3 us
    dot_general x1, matrix products, body(): jnp.einsum('ijkr,ijrf->jkf', v_factors, back, preferred_element_type=jnp....  7.69 us
    dot_general x1, matrix products, body(): jnp.einsum('ijkr,ijrf->ikf', u_factors, coef, preferred_element_type=jnp....  6.62 us
    ppermute x2, waiting for transfers between devices, body(): lax.ppermute(going_up, 'row', [(d, (d + 1) % ways) for d in range(ways)])  5.52 us
    ppermute x2, starting transfers between devices, padded_2(): lax.ppermute(lax.slice_in_dim(block, 0, width, axis=dim), axis, backward)  4.79 us
    ppermute x2, starting transfers between devices, padded_2(): lax.ppermute(lax.slice_in_dim(block, block.shape[dim] - width, None, axis...  4.3 us
  transfers between devices with their start and end apart: 9, of which 8 were waited for; matrix products, arithmetic and copies ran while one was open for 1% of the time, Pallas kernels for 0%

profile of v1, /device:TPU:1, one launch (start us, length us, event | category | flops | bytes accessed | tf_op | source)
XLA Modules:
  0.0 168.1 jit_solution(2017379269655971587)
XLA Ops:
  6.7 1.0 constant_dynamic-update-slice_fusion.3
  7.7 2.2 %collective-permute-start = (bf16[4,2,64,128]{3,2,1,0:T(8,128)(2,1)S(1)}, bf16[4,2,64,128]{3,2,1,0:T(8,128)(2,1)S(1)}, u32[]{:S(2)}, u32[]{:S(2)}) collective-permute-start(bf16[4,2,64,128]{3,2,1,0:T(8,128)(2,1)S(1)} %get-tuple-element.6), channel_id=1, source_target_pairs={{0,8},{8,16},{16,24},{24,0},{1,9},{9,17},{17,25},{25,1},{2,10},{10... | collective-permute-start | bytes 393224 | tf_op jit(solution)/shard_map/ppermute | solution.py:47
  9.8 2.1 %collective-permute-start.1 = (bf16[4,2,64,128]{3,2,1,0:T(8,128)(2,1)S(1)}, bf16[4,2,64,128]{3,2,1,0:T(8,128)(2,1)S(1)}, u32[]{:S(2)}, u32[]{:S(2)}) collective-permute-start(bf16[4,2,64,128]{3,2,1,0:T(8,128)(2,1)S(1)} %get-tuple-element.6), channel_id=1, source_target_pairs={{0,24},{8,0},{16,8},{24,16},{1,25},{9,1},{17,9},{25,17},{2,26},{10... | collective-permute-start | bytes 393224 | tf_op jit(solution)/shard_map/ppermute | solution.py:50
  11.9 0.8 fusion.28
  12.7 2.4 %collective-permute-done = bf16[4,2,64,128]{3,2,1,0:T(8,128)(2,1)S(1)} collective-permute-done((bf16[4,2,64,128]{3,2,1,0:T(8,128)(2,1)S(1)}, bf16[4,2,64,128]{3,2,1,0:T(8,128)(2,1)S(1)}, u32[]{:S(2)}, u32[]{:S(2)}) %collective-permute-start) | collective-permute-done | bytes 131104 | tf_op jit(solution)/shard_map/ppermute | solution.py:47
  15.1 2.4 %collective-permute-done.1 = bf16[4,2,64,128]{3,2,1,0:T(8,128)(2,1)S(1)} collective-permute-done((bf16[4,2,64,128]{3,2,1,0:T(8,128)(2,1)S(1)}, bf16[4,2,64,128]{3,2,1,0:T(8,128)(2,1)S(1)}, u32[]{:S(2)}, u32[]{:S(2)}) %collective-permute-start.1) | collective-permute-done | bytes 131104 | tf_op jit(solution)/shard_map/ppermute | solution.py:50
  17.5 3.2 %collective-permute-done.2 = bf16[4,2,64,128]{3,2,1,0:T(8,128)(2,1)S(1)} collective-permute-done((bf16[4,2,64,128]{3,2,1,0:T(8,128)(2,1)S(1)}, bf16[4,2,64,128]{3,2,1,0:T(8,128)(2,1)S(1)}, u32[]{:S(2)}, u32[]{:S(2)}) %collective-permute-start.2) | collective-permute-done | bytes 131104 | tf_op jit(solution)/shard_map/ppermute | solution.py:47
  20.7 6.6 %convolution_bitcast_fusion = f32[5,1024,128]{1,2,0:T(8,128)S(1)} fusion(bf16[5,2,1024,256]{3,2,1,0:T(8,128)(2,1)} %param.6, bf16[2,1024,128,1]{2,1,0,3:T(8,128)(2,1)S(1)} %bitcast.37, bf16[5,2,1024,256]{3,2,1,0:T(8,128)(2,1)} %param.7, f32[5,2,256]{2,1,0:T(2,128)S(1)} %copy.8), kind=kOutput, calls=%fused_computation.7 | convolution fusion | flops 1342832640 | bytes 13641728 | tf_op jit(solution)/shard_map/ijkr,ijrf->ikf/dot_general | solution.py:60
  27.3 2.1 %copy.9 = f32[5,1024,128]{2,1,0:T(8,128)} copy(f32[5,1024,128]{1,2,0:T(8,128)S(1)} %convolution_bitcast_fusion) | data formatting | bytes 5242880 | tf_op jit(solution)/shard_map/ijkr,ijrf->ikf/dot_general | solution.py:60
  29.6 65.9 %all-reduce.4.cloned.1.call-done = f32[5120,128]{1,0:T(8,128)} async-done(((f32[5120,128]{1,0:T(8,128)}), f32[5120,128]{1,0:T(8,128)}) %all-reduce.4.cloned.1.call-update) | async-done | bytes 2621456 | tf_op jit(solution)/shard_map/psum | solution.py:64
  95.5 2.0 %subtract_convert_fusion = bf16[5120,128]{1,0:T(8,128)(2,1)S(1)} fusion(f32[5120,128]{1,0:T(8,128)} %all-reduce.4.cloned.1.call-done, bf16[5120,128]{1,0:T(8,128)(2,1)S(1)} %copy-done), kind=kLoop, calls=%fused_computation.4 | loop fusion | flops 1966080 | bytes 5242880 | tf_op jit(solution)/shard_map/convert_element_type | solution.py:65
  97.5 7.7 %fusion.8 = f32[2,1024,128]{1,2,0:T(8,128)} fusion(bf16[5,2,1024,256]{3,2,1,0:T(8,128)(2,1)} %param.7, bf16[5,1024,128,1]{2,1,0,3:T(8,128)(2,1)S(1)} %bitcast.38, bf16[5,2,1024,256]{3,2,1,0:T(8,128)(2,1)} %param.6, f32[5,2,256]{2,0,1:T(8,128)S(1)} %fusion.28), kind=kOutput, calls=%fused_computation.12 | convolution fusion | flops 1342832640 | bytes 12855296 | tf_op jit(solution)/shard_map/ijkr,ijrf->jkf/dot_general | solution.py:69
  105.2 2.6 %copy.11 = f32[2,1024,128]{2,1,0:T(8,128)} copy(f32[2,1024,128]{1,2,0:T(8,128)} %fusion.8) | data formatting | bytes 2097152 | tf_op jit(solution)/shard_map/ijkr,ijrf->jkf/dot_general | solution.py:69
  107.8 27.3 %reduce-scatter.2.cloned.1.call-done = f32[512,128]{1,0:T(8,128)} async-done(((f32[2048,128]{1,0:T(8,128)}), f32[512,128]{1,0:T(8,128)}) %reduce-scatter.2.cloned.1.call-update) | async-done | bytes 262160 | tf_op jit(solution)/shard_map/reduce_scatter | solution.py:71
  135.0 1.0 sub.59
  136.0 1.3 collective-permute-start.3
  137.3 1.3 collective-permute-start.4
  138.6 0.6 collective-permute-done.3
  139.3 4.7 %collective-permute-done.4 = f32[2,2,64,128]{3,2,1,0:T(8,128)S(1)} collective-permute-done((f32[2,2,64,128]{3,2,1,0:T(8,128)S(1)}, f32[2,2,64,128]{3,2,1,0:T(8,128)S(1)}, u32[]{:S(2)}, u32[]{:S(2)}) %collective-permute-start.4) | collective-permute-done | bytes 131104 | tf_op jit(solution)/shard_map/ppermute | solution.py:18
  144.0 3.5 %collective-permute-start.6 = (f32[8,2,64,128]{3,2,1,0:T(8,128)S(1)}, f32[8,2,64,128]{3,2,1,0:T(8,128)S(1)}, u32[]{:S(2)}, u32[]{:S(2)}) collective-permute-start(f32[8,2,64,128]{3,2,1,0:T(8,128)S(1)} %pad_maximum_fusion.7), channel_id=1, source_target_pairs={{1,0},{2,1},{3,2},{4,3},{5,4},{6,5},{7,6},{9,8},{10,9},{11,10},{12... | collective-permute-start | bytes 1572872 | tf_op jit(solution)/shard_map/ppermute | solution.py:18
  147.5 3.0 %collective-permute-start.5 = (f32[8,2,64,128]{3,2,1,0:T(8,128)S(1)}, f32[8,2,64,128]{3,2,1,0:T(8,128)S(1)}, u32[]{:S(2)}, u32[]{:S(2)}) collective-permute-start(f32[8,2,64,128]{3,2,1,0:T(8,128)S(1)} %pad_maximum_fusion.7), channel_id=1, source_target_pairs={{0,1},{1,2},{2,3},{3,4},{4,5},{5,6},{6,7},{8,9},{9,10},{10,11},{11... | collective-permute-start | bytes 1572872 | tf_op jit(solution)/shard_map/ppermute | solution.py:15
  150.7 7.6 %collective-permute-done.6 = f32[8,2,64,128]{3,2,1,0:T(8,128)S(1)} collective-permute-done((f32[8,2,64,128]{3,2,1,0:T(8,128)S(1)}, f32[8,2,64,128]{3,2,1,0:T(8,128)S(1)}, u32[]{:S(2)}, u32[]{:S(2)}) %collective-permute-start.6) | collective-permute-done | bytes 524320 | tf_op jit(solution)/shard_map/ppermute | solution.py:18
  158.5 1.6 add_select_fusion
  160.1 1.1 multiply_add_fusion
  (21 shorter events, 0.6 us)
Async XLA Ops:
  6.5 88.9 %all-reduce.4.cloned.1.call-start = ((), (), s32[]{:S(2)}) async-start(), calls=%async_computation.1 | async-start | bytes 5242880 | tf_op jit(solution)/shard_map/psum | solution.py:64
  7.7 7.4 %collective-permute-start = (bf16[4,2,64,128]{3,2,1,0:T(8,128)(2,1)S(1)}, bf16[4,2,64,128]{3,2,1,0:T(8,128)(2,1)S(1)}, u32[]{:S(2)}, u32[]{:S(2)}) collective-permute-start(bf16[4,2,64,128]{3,2,1,0:T(8,128)(2,1)S(1)} %get-tuple-element.6), channel_id=1, source_target_pairs={{0,8},{8,16},{16,24},{24,0},{1,9},{9,17},{17,25},{25,1},{2,10},{10... | collective-permute-start | bytes 393224 | tf_op jit(solution)/shard_map/ppermute | solution.py:47
  9.8 7.7 %collective-permute-start.1 = (bf16[4,2,64,128]{3,2,1,0:T(8,128)(2,1)S(1)}, bf16[4,2,64,128]{3,2,1,0:T(8,128)(2,1)S(1)}, u32[]{:S(2)}, u32[]{:S(2)}) collective-permute-start(bf16[4,2,64,128]{3,2,1,0:T(8,128)(2,1)S(1)} %get-tuple-element.6), channel_id=1, source_target_pairs={{0,24},{8,0},{16,8},{24,16},{1,25},{9,1},{17,9},{25,17},{2,26},{10... | collective-permute-start | bytes 393224 | tf_op jit(solution)/shard_map/ppermute | solution.py:50
  15.1 5.6 %collective-permute-start.2 = (bf16[4,2,64,128]{3,2,1,0:T(8,128)(2,1)S(1)}, bf16[4,2,64,128]{3,2,1,0:T(8,128)(2,1)S(1)}, u32[]{:S(2)}, u32[]{:S(2)}) collective-permute-start(bf16[4,2,64,128]{3,2,1,0:T(8,128)(2,1)S(1)} %collective-permute-done), channel_id=1, source_target_pairs={{0,8},{8,16},{16,24},{24,0},{1,9},{9,17},{17,25},{25,1},{2,10},{10... | collective-permute-start | bytes 393224 | tf_op jit(solution)/shard_map/ppermute | solution.py:47
  29.5 66.0 %copy-start = (bf16[5120,128]{1,0:T(8,128)(2,1)S(1)}, bf16[5120,128]{1,0:T(8,128)(2,1)}, u32[]{:S(2)}) copy-start(bf16[5120,128]{1,0:T(8,128)(2,1)} %param.9) | copy-start | bytes 3932164
  29.5 105.5 %reduce-scatter.2.cloned.1.call-start = ((), (), s32[]{:S(2)}) async-start(), calls=%async_computation.2 | async-start | bytes 1310720 | tf_op jit(solution)/shard_map/reduce_scatter | solution.py:71
  105.2 29.9 %copy-start.1 = (f32[4,2,64,128]{3,2,1,0:T(8,128)S(1)}, f32[4,2,64,128]{3,2,1,0:T(8,128)}, u32[]{:S(2)}) copy-start(f32[4,2,64,128]{3,2,1,0:T(8,128)} %param.5) | copy-start | bytes 786436
  136.0 3.2 %collective-permute-start.3 = (f32[2,2,64,128]{3,2,1,0:T(8,128)S(1)}, f32[2,2,64,128]{3,2,1,0:T(8,128)S(1)}, u32[]{:S(2)}, u32[]{:S(2)}) collective-permute-start(f32[2,2,64,128]{3,2,1,0:T(8,128)S(1)} %get-tuple-element.7), channel_id=1, source_target_pairs={{0,8},{8,16},{16,24},{1,9},{9,17},{17,25},{2,10},{10,18},{18,26},{... | collective-permute-start | bytes 393224 | tf_op jit(solution)/shard_map/ppermute | solution.py:15
  137.3 6.6 %collective-permute-start.4 = (f32[2,2,64,128]{3,2,1,0:T(8,128)S(1)}, f32[2,2,64,128]{3,2,1,0:T(8,128)S(1)}, u32[]{:S(2)}, u32[]{:S(2)}) collective-permute-start(f32[2,2,64,128]{3,2,1,0:T(8,128)S(1)} %get-tuple-element.8), channel_id=1, source_target_pairs={{8,0},{16,8},{24,16},{9,1},{17,9},{25,17},{10,2},{18,10},{26,18},{... | collective-permute-start | bytes 393224 | tf_op jit(solution)/shard_map/ppermute | solution.py:18
  144.0 14.2 %collective-permute-start.6 = (f32[8,2,64,128]{3,2,1,0:T(8,128)S(1)}, f32[8,2,64,128]{3,2,1,0:T(8,128)S(1)}, u32[]{:S(2)}, u32[]{:S(2)}) collective-permute-start(f32[8,2,64,128]{3,2,1,0:T(8,128)S(1)} %pad_maximum_fusion.7), channel_id=1, source_target_pairs={{1,0},{2,1},{3,2},{4,3},{5,4},{6,5},{7,6},{9,8},{10,9},{11,10},{12... | collective-permute-start | bytes 1572872 | tf_op jit(solution)/shard_map/ppermute | solution.py:18
  147.5 10.7 %collective-permute-start.5 = (f32[8,2,64,128]{3,2,1,0:T(8,128)S(1)}, f32[8,2,64,128]{3,2,1,0:T(8,128)S(1)}, u32[]{:S(2)}, u32[]{:S(2)}) collective-permute-start(f32[8,2,64,128]{3,2,1,0:T(8,128)S(1)} %pad_maximum_fusion.7), channel_id=1, source_target_pairs={{0,1},{1,2},{2,3},{3,4},{4,5},{5,6},{6,7},{8,9},{9,10},{10,11},{11... | collective-permute-start | bytes 1572872 | tf_op jit(solution)/shard_map/ppermute | solution.py:15
Sparse Core Ops, SparseCore 0:
  29.6 65.7 all-reduce.3
  107.9 27.1 reduce-scatter.1
